TPU v7x, 32 devices: a whole 2x2x4 slice. The times are simulated.
32 devices in a mesh: layer: 4 (over y, core), latent: 8 (over z, x).
Axes of the slice: x: 2, y: 2, z: 4, core: 2. Of those that a mesh axis runs over, the one named last changes fastest.
Arguments:
- inputs: bfloat16 [4, 128, 4096], P('layer', 'latent'), may hold values from -6 to 6
- targets: bfloat16 [4, 128, 4096], P('layer', 'latent'), may hold values from -6 to 6
- w_enc: bfloat16 [4, 4096, 8192], P('layer', None, 'latent'), may hold values from -0.09375 to 0.09375
- b_enc: float32 [4, 8192], P('layer', 'latent'), may hold values from -3 to 3
- w_dec: bfloat16 [4, 4, 8192, 4096], P('layer', None, 'latent'), may hold values from -0.03125 to 0.03125
- b_dec: float32 [4, 4096], P('layer'), may hold values from -3 to 3
Outputs:
- grad_enc: bfloat16 [4, 4096, 8192], P('layer', None, 'latent')
- grad_benc: float32 [4, 8192], P('layer', 'latent')
- grad_dec: bfloat16 [4, 4, 8192, 4096], P('layer', None, 'latent')
- grad_bdec: float32 [4, 4096], P('layer')
All inputs are finite; a program needn't handle non-finite values.
Results may differ from a plain program's by a relative error of at most 0.0057.
Values may be sent and summed in bfloat16 or wider, within the bound.
A program may use at most 192 MiB of HBM per device.

v0:
```python
import jax
import jax.numpy as jnp
from jax import lax
from jax.sharding import PartitionSpec as P

penalty = 0.5
eps = 1e-06


def local(inputs, targets, w_enc, b_enc, w_dec, b_dec):
    source = lax.axis_index("layer")
    depth = w_dec.shape[1]
    whole = lax.all_gather(inputs[0], "latent", axis=0, tiled=True)
    pre = jnp.dot(whole, w_enc[0], preferred_element_type=jnp.float32) + b_enc[0]
    positive = jnp.maximum(pre, 0.0)
    act = (positive * positive).astype(jnp.bfloat16)
    valid = (jnp.arange(depth, dtype=jnp.int32) >= source).astype(jnp.float32)
    partial_value = (
        jnp.einsum("nk,tkd->tnd", act, w_dec[0], preferred_element_type=jnp.float32)
        * valid[:, None, None]
    )
    spread = lax.psum_scatter(partial_value, "layer", scatter_dimension=0, tiled=True)
    recon = lax.psum_scatter(spread, "latent", scatter_dimension=1, tiled=True)
    error = recon[0] + b_dec[0] - targets[0].astype(jnp.float32)
    grad_bdec = lax.psum(jnp.sum(error, axis=0), "latent")[None, :]
    err_low = error.astype(jnp.bfloat16)[None]
    stacked = lax.all_gather(err_low, "latent", axis=1, tiled=True)
    errors = lax.all_gather(stacked, "layer", axis=0, tiled=True)
    errors = jnp.where(valid[:, None, None] > 0.0, errors, jnp.zeros_like(errors))
    decoders = w_dec[0]
    squares = jnp.sum(jnp.square(decoders.astype(jnp.float32)), axis=2)
    norms = jnp.sqrt(jnp.sum(squares * valid[:, None], axis=0) + eps)
    back = jnp.einsum("tnd,tkd->nk", errors, decoders, preferred_element_type=jnp.float32)
    d_act = back + penalty * norms[None, :]
    d_pre = d_act * 2.0 * positive
    grad_benc = jnp.sum(d_pre, axis=0)[None, :]
    d_low = d_pre.astype(jnp.bfloat16)
    grad_enc = lax.dot_general(
        whole, d_low, (((0,), (0,)), ((), ())), preferred_element_type=jnp.float32
    ).astype(jnp.bfloat16)[None]
    act_total = jnp.sum(act.astype(jnp.float32), axis=0)
    scale = penalty * act_total / norms
    grad_mse = jnp.einsum("nk,tnd->tkd", act, errors, preferred_element_type=jnp.float32)
    shrink = valid[:, None, None] * scale[None, :, None] * decoders.astype(jnp.float32)
    grad_dec = (grad_mse + shrink).astype(jnp.bfloat16)[None]
    return (grad_enc, grad_benc, grad_dec, grad_bdec)


def solution(mesh):
    placed = (
        P("layer", "latent", None),
        P("layer", "latent", None),
        P("layer", None, "latent"),
        P("layer", "latent"),
        P("layer", None, "latent", None),
        P("layer", None),
    )
    return jax.shard_map(
        local,
        mesh=mesh,
        in_specs=placed,
        out_specs=(
            P("layer", None, "latent"),
            P("layer", "latent"),
            P("layer", None, "latent", None),
            P("layer", None),
        ),
        check_vma=False,
    )
```

profile of v0, /device:TPU:0, one launch (start us, length us, event | category | flops | bytes accessed | tf_op | source)
XLA Modules:
  0.0 456.9 jit_solution(2697420618974324879)
XLA Ops:
  7.2 0.0 all-gather.9.cloned.1.call-start
  7.2 0.7 all-gather.9.cloned.1.call-update
  7.9 0.0 reduce-scatter.3.cloned.1.call-start
  8.0 45.2 %all-gather.9.cloned.1.call-done = bf16[1,128,4096]{2,1,0:T(8,128)(2,1)} async-done(((bf16[1,16,4096]{2,1,0:T(8,128)(2,1)}), bf16[1,128,4096]{2,1,0:T(8,128)(2,1)}) %all-gather.9.cloned.1.call-update) | async-done | bytes 1048592 | tf_op jit(solution)/shard_map/all_gather | solution.py:13
  53.1 4.9 %convert_reduce_fusion = (f32[1024]{0:T(1024)S(1)}, f32[128,1024]{1,0:T(8,128)S(1)}) fusion(f32[1024]{0:T(1024)} %bitcast.82, bf16[1,4096,1024]{2,1,0:T(8,128)(2,1)} %param.8, bf16[1,128,4096]{2,1,0:T(8,128)(2,1)} %all-gather.9.cloned.1.call-done), kind=kOutput, calls=%fused_computation.23 | convolution fusion | flops 1074527232 | bytes 9969664 | tf_op jit(solution)/shard_map/dot_general | solution.py:14
  58.0 18.5 %multiply_bitcast_fusion = f32[4,128,4096]{2,1,0:T(8,128)} fusion(f32[4]{0:T(128)S(1)} %compare_convert_fusion, bf16[1,4,1024,4096]{3,2,1,0:T(8,128)(2,1)} %param.10, f32[128,1024]{1,0:T(8,128)S(1)} %get-tuple-element.15), kind=kOutput, calls=%fused_computation.13 | convolution fusion | flops 4297326592 | bytes 42467344 | tf_op jit(solution)/shard_map/nk,tkd->tnd/dot_general | solution.py:19
  76.5 0.0 copy-start.2
  76.5 0.0 copy-start.3
  76.5 0.0 reduce-scatter.3.cloned.1.call-update
  76.6 0.0 reduce-scatter.5.cloned.1.call-start
  76.6 70.2 %reduce-scatter.3.cloned.1.call-done = f32[1,128,4096]{2,1,0:T(8,128)} async-done(((f32[4,128,4096]{2,1,0:T(8,128)}), f32[1,128,4096]{2,1,0:T(8,128)}) %reduce-scatter.3.cloned.1.call-update) | async-done | bytes 2097168 | tf_op jit(solution)/shard_map/reduce_scatter | solution.py:22
  146.9 0.0 reduce-scatter.5.cloned.1.call-update
  146.9 0.0 all-gather.5.cloned.1.call-start
  146.9 72.2 %reduce-scatter.5.cloned.1.call-done = f32[1,16,4096]{2,1,0:T(8,128)} async-done(((f32[1,128,4096]{2,1,0:T(8,128)}), f32[1,16,4096]{2,1,0:T(8,128)}) %reduce-scatter.5.cloned.1.call-update) | async-done | bytes 262160 | tf_op jit(solution)/shard_map/reduce_scatter | solution.py:23
  219.2 0.0 copy-done.2
  219.2 0.0 copy-done.3
  219.2 1.6 fusion.32
  220.8 0.0 all-gather.5.cloned.1.call-update
  220.8 0.0 all-gather.7.cloned.1.call-start
  220.9 40.2 %all-gather.5.cloned.1.call-done = bf16[1,128,4096]{2,1,0:T(8,128)(2,1)} async-done(((bf16[1,16,4096]{2,1,0:T(8,128)(2,1)}), bf16[1,128,4096]{2,1,0:T(8,128)(2,1)}) %all-gather.5.cloned.1.call-update) | async-done | bytes 1048592 | tf_op jit(solution)/shard_map/all_gather | solution.py:27
  261.1 0.0 all-gather.7.cloned.1.call-update
  261.1 40.6 %copy.16 = bf16[1,4,1024,4096]{2,3,1,0:T(8,128)(2,1)} copy(bf16[1,4,1024,4096]{3,2,1,0:T(8,128)(2,1)} %param.10) | data formatting | bytes 67108864 | tf_op args[4]
  301.6 0.0 copy-start.1
  301.7 11.7 %fusion = f32[4,1024]{1,0:T(4,128)S(1)} fusion(bf16[1,4,1024,4096]{2,3,1,0:T(8,128)(2,1)} %copy.16), kind=kLoop, calls=%fused_computation.2 | loop fusion | flops 50327552 | bytes 33570816 | tf_op jit(solution)/shard_map/reduce_sum | solution.py:31
  313.4 0.1 multiply_reduce_fusion
  313.5 0.1 broadcast_multiply_fusion
  313.5 0.0 copy-done.1
  313.5 0.1 fusion.34
  313.6 35.7 %psum.7 = f32[1,4096]{1,0:T(1,128)} all-reduce(f32[1,4096]{1,0:T(1,128)S(1)} %bitcast.81), channel_id=1, replica_groups=mesh['layer'=4,'latent'=8] {'latent'}, use_global_device_ids=true, to_apply=%region_7.8 | all-reduce | flops 4096 | bytes 32768 | tf_op jit(solution)/shard_map/psum | solution.py:25
  349.3 0.0 all-gather.7.cloned.1.call-done
  349.3 25.4 %fusion.7 = bf16[1,4,1024,4096]{2,3,1,0:T(8,128)(2,1)} fusion(bf16[1,4,1024,4096]{2,3,1,0:T(8,128)(2,1)} %copy.16, f32[4,1024]{1,0:T(4,128)S(1)} %broadcast_multiply_fusion, bf16[4,128,4096]{2,1,0:T(8,128)(2,1)} %all-gather.7.cloned.1.call-done, pred[4]{0:T(512)(128)(4,1)S(1)} %broadcast_compare_fusion, f32[128,1024]{1,0:T(8,128)S(1)} %get-tuple-element.15), kind=kOutput, calls=%fused_computation.9 | convolution fusion | flops 4364435456 | bytes 71843840 | tf_op jit(solution)/shard_map/nk,tnd->tkd/dot_general | solution.py:43
  374.7 40.5 %copy.21 = bf16[1,4,1024,4096]{3,2,1,0:T(8,128)(2,1)} copy(bf16[1,4,1024,4096]{2,3,1,0:T(8,128)(2,1)} %fusion.7) | data formatting | bytes 67108864
  415.2 0.0 copy-start
  415.2 17.6 %fusion.40 = (f32[1024]{0:T(1024)}, bf16[128,1024]{1,0:T(8,128)(2,1)S(1)}) fusion(f32[128,1024]{1,0:T(8,128)S(1)} %get-tuple-element.15, f32[1024]{0:T(1024)S(1)} %get-tuple-element.13, bf16[1,4,1024,4096]{3,2,1,0:T(8,128)(2,1)} %param.10, bf16[4,128,4096]{2,1,0:T(8,128)(2,1)} %all-gather.7.cloned.1.call-done, pred[4]{0:T(512)(128)(4,1)S(1)} %broadcast_compare_fusion), kind=kOutput, calls=%fused_computation.42 | convolution fusion | flops 4297718784 | bytes 38543364 | tf_op jit(solution)/shard_map/tnd,tkd->nk/dot_general | solution.py:33
  432.8 0.0 copy-done
  432.8 5.6 %convert_bitcast_fusion = bf16[1,4096,1024]{1,2,0:T(8,128)(2,1)} fusion(bf16[1,128,4096]{2,1,0:T(8,128)(2,1)S(1)} %copy-done, bf16[128,1024]{1,0:T(8,128)(2,1)S(1)} %get-tuple-element.17), kind=kOutput, calls=%fused_computation.12 | convolution fusion | flops 1077936128 | bytes 9699328 | tf_op jit(solution)/shard_map/dot_general | solution.py:38
  438.4 11.9 %copy.20 = bf16[1,4096,1024]{2,1,0:T(8,128)(2,1)} copy(bf16[1,4096,1024]{1,2,0:T(8,128)(2,1)} %convert_bitcast_fusion) | data formatting | bytes 16777216
  (3 shorter events, 0.0 us)
Async XLA Ops:
  7.2 46.0 %all-gather.9.cloned.1.call-start = ((), (), s32[]{:S(2)}) async-start(), calls=%async_computation.6 | async-start | bytes 1179648 | tf_op jit(solution)/shard_map/all_gather | solution.py:13
  7.9 139.0 %reduce-scatter.3.cloned.1.call-start = ((), (), s32[]{:S(2)}) async-start(), calls=%async_computation.2 | async-start | bytes 10485760 | tf_op jit(solution)/shard_map/reduce_scatter | solution.py:22
  76.5 142.6 %copy-start.2 = (bf16[1,16,4096]{2,1,0:T(8,128)(2,1)S(1)}, bf16[1,16,4096]{2,1,0:T(8,128)(2,1)}, u32[]{:S(2)}) copy-start(bf16[1,16,4096]{2,1,0:T(8,128)(2,1)} %param.7) | copy-start | bytes 393220
  76.5 142.6 %copy-start.3 = (f32[1,4096]{1,0:T(1,128)S(1)}, f32[1,4096]{1,0:T(1,128)}, u32[]{:S(2)}) copy-start(f32[1,4096]{1,0:T(1,128)} %param.11) | copy-start | bytes 49156
  76.6 142.6 %reduce-scatter.5.cloned.1.call-start = ((), (), s32[]{:S(2)}) async-start(), calls=%async_computation.3 | async-start | bytes 2359296 | tf_op jit(solution)/shard_map/reduce_scatter | solution.py:23
  146.9 114.2 %all-gather.5.cloned.1.call-start = ((), (), s32[]{:S(2)}) async-start(), calls=%async_computation.4 | async-start | bytes 1179648 | tf_op jit(solution)/shard_map/all_gather | solution.py:27
  220.8 128.5 %all-gather.7.cloned.1.call-start = ((), (), s32[]{:S(2)}) async-start(), calls=%async_computation.5 | async-start | bytes 5242880 | tf_op jit(solution)/shard_map/all_gather | solution.py:28
  301.6 11.9 %copy-start.1 = (f32[1,16,4096]{2,1,0:T(8,128)S(1)}, f32[1,16,4096]{2,1,0:T(8,128)}, u32[]{:S(2)}) copy-start(f32[1,16,4096]{2,1,0:T(8,128)} %reduce-scatter.5.cloned.1.call-done) | copy-start | bytes 786436
  415.2 17.6 %copy-start = (bf16[1,128,4096]{2,1,0:T(8,128)(2,1)S(1)}, bf16[1,128,4096]{2,1,0:T(8,128)(2,1)}, u32[]{:S(2)}) copy-start(bf16[1,128,4096]{2,1,0:T(8,128)(2,1)} %all-gather.9.cloned.1.call-done) | copy-start | bytes 3145732
Sparse Core Ops, SparseCore 0:
  10.1 42.9 all-gather.8
  76.7 70.1 reduce-scatter.2
  150.4 68.7 reduce-scatter.4
  221.7 39.2 all-gather.4
  262.5 33.1 all-gather.6
where the time goes:
time: 459 us; the launch traced here: 457 us
  waiting for transfers between devices  229 us (50%)
  local copies, waits for them, and re-layouts  93 us (20%)
  matrix products  72 us (16%)
  blocking collectives  35.7 us (8%)
  between operations  13.8 us (3%)
  other arithmetic  13.6 us (3%)
    unnamed x11, local copies, waits for them, and re-layouts  93 us
    reduce_scatter x1, waiting for transfers between devices, local(): recon = lax.psum_scatter(spread, 'latent', scatter_dimension=1, tiled=True)  72.2 us
    reduce_scatter x1, waiting for transfers between devices, local(): lax.psum_scatter(partial_value, 'layer', scatter_dimension=0, tiled=True)  70.2 us
    all_gather x1, waiting for transfers between devices, local(): whole = lax.all_gather(inputs[0], 'latent', axis=0, tiled=True)  45.2 us
    all_gather x1, waiting for transfers between devices, local(): stacked = lax.all_gather(err_low, 'latent', axis=1, tiled=True)  40.2 us
    psum x1, blocking collectives, local(): grad_bdec = lax.psum(jnp.sum(error, axis=0), 'latent')[None, :]  35.7 us
    dot_general x1, matrix products, local(): jnp.einsum('nk,tnd->tkd', act, errors, preferred_element_type=jnp.float32)  25.4 us
    dot_general x1, matrix products, local(): jnp.einsum('nk,tkd->tnd', act, w_dec[0], preferred_element_type=jnp.float32)  18.5 us
  transfers between devices with their start and end apart: 5, of which 4 were waited for; matrix products, arithmetic and copies ran while one was open for 11% of the time, Pallas kernels for 0%

commit v1 on v0

--- a/solution.py
+++ b/solution.py
@@ -25,7 +25,22 @@
     grad_bdec = lax.psum(jnp.sum(error, axis=0), "latent")[None, :]
     err_low = error.astype(jnp.bfloat16)[None]
     stacked = lax.all_gather(err_low, "latent", axis=1, tiled=True)
-    errors = lax.all_gather(stacked, "layer", axis=0, tiled=True)
+    size, index, rows = (lax.axis_size("layer"), lax.axis_index("layer"), stacked.shape[0])
+    upward = [(i, (i + 1) % size) for i in range(size)]
+    left = [(i, (i - 1) % size) for i in range(size)]
+    out = jnp.zeros((*stacked.shape[:0], size * rows, *stacked.shape[0 + 1 :]), stacked.dtype)
+    out = lax.dynamic_update_slice_in_dim(out, stacked, index * rows, axis=0)
+    from_left = from_right = stacked
+    half = size // 2
+    for step in range(1, half + 1):
+        from_left = lax.ppermute(from_left, "layer", upward)
+        out = lax.dynamic_update_slice_in_dim(out, from_left, (index - step) % size * rows, axis=0)
+        if step < size - half:
+            from_right = lax.ppermute(from_right, "layer", left)
+            out = lax.dynamic_update_slice_in_dim(
+                out, from_right, (index + step) % size * rows, axis=0
+            )
+    errors = out
     errors = jnp.where(valid[:, None, None] > 0.0, errors, jnp.zeros_like(errors))
     decoders = w_dec[0]
     squares = jnp.sum(jnp.square(decoders.astype(jnp.float32)), axis=2)

time: 459 us -> 438 us (0.954)
  waiting for transfers between devices: 229 us -> 194 us
  local copies, waits for them, and re-layouts: 93 us -> 105 us
    all_gather x1, waiting for transfers between devices: 40.2 us -> 0.01 us  [local(): stacked = lax.all_gather(err_low, 'latent', axis=1, tiled=True)]
    ppermute x0 -> x3, waiting for transfers between devices: none -> 5.6 us  [the longest x2 5.6 us: local(): from_left = lax.ppermute(from_left, 'layer', upward)]
    ppermute x0 -> x3, local copies, waits for them, and re-layouts: none -> 4.84 us  [the longest x2 3.22 us: local(): from_left = lax.ppermute(from_left, 'layer', upward)]
    unnamed x11 -> x13, local copies, waits for them, and re-layouts: 93 us -> 93.1 us
  transfers between devices with their start and end apart: 5 -> 7, of which waited for: 4 -> 4; matrix products, arithmetic and copies ran while one was open for 11% -> 14% of each run, Pallas kernels for 0% -> 0%
where the time goes in v1:
time: 438 us; the launch traced here: 436 us
  waiting for transfers between devices  194 us (44%)
  local copies, waits for them, and re-layouts  105 us (24%)
  matrix products  71.2 us (16%)
  blocking collectives  35.4 us (8%)
  between operations  13.9 us (3%)
  other arithmetic  13.6 us (3%)
    unnamed x13, local copies, waits for them, and re-layouts  93.1 us
    reduce_scatter x1, waiting for transfers between devices, local(): recon = lax.psum_scatter(spread, 'latent', scatter_dimension=1, tiled=True)  72.2 us
    reduce_scatter x1, waiting for transfers between devices, local(): lax.psum_scatter(partial_value, 'layer', scatter_dimension=0, tiled=True)  70.2 us
    all_gather x1, waiting for transfers between devices, local(): whole = lax.all_gather(inputs[0], 'latent', axis=0, tiled=True)  45.2 us
    psum x1, blocking collectives, local(): grad_bdec = lax.psum(jnp.sum(error, axis=0), 'latent')[None, :]  35.4 us
    dot_general x1, matrix products, local(): jnp.einsum('nk,tnd->tkd', act, errors, preferred_element_type=jnp.float32)  24.5 us
    dot_general x1, matrix products, local(): jnp.einsum('nk,tkd->tnd', act, w_dec[0], preferred_element_type=jnp.float32)  18.5 us
    dot_general x1, matrix products, local(): jnp.einsum('tnd,tkd->nk', errors, decoders, preferred_element_type=jnp.fl...  17.8 us
  transfers between devices with their start and end apart: 7, of which 4 were waited for; matrix products, arithmetic and copies ran while one was open for 14% of the time, Pallas kernels for 0%

profile of v1, /device:TPU:0, one launch (start us, length us, event | category | flops | bytes accessed | tf_op | source)
XLA Modules:
  0.0 435.6 jit_solution(2208198624674386164)
XLA Ops:
  7.2 0.0 all-gather.6.cloned.1.call-start
  7.2 0.7 all-gather.6.cloned.1.call-update
  7.9 0.0 reduce-scatter.3.cloned.1.call-start
  8.0 45.2 %all-gather.6.cloned.1.call-done = bf16[1,128,4096]{2,1,0:T(8,128)(2,1)} async-done(((bf16[1,16,4096]{2,1,0:T(8,128)(2,1)}), bf16[1,128,4096]{2,1,0:T(8,128)(2,1)}) %all-gather.6.cloned.1.call-update) | async-done | bytes 1048592 | tf_op jit(solution)/shard_map/all_gather | solution.py:13
  53.1 4.9 %convert_reduce_fusion = (f32[1024]{0:T(1024)S(1)}, f32[128,1024]{1,0:T(8,128)S(1)}) fusion(f32[1024]{0:T(1024)} %bitcast.82, bf16[1,4096,1024]{2,1,0:T(8,128)(2,1)} %param.8, bf16[1,128,4096]{2,1,0:T(8,128)(2,1)} %all-gather.6.cloned.1.call-done), kind=kOutput, calls=%fused_computation.23 | convolution fusion | flops 1074527232 | bytes 9969664 | tf_op jit(solution)/shard_map/dot_general | solution.py:14
  58.0 18.5 %multiply_bitcast_fusion = f32[4,128,4096]{2,1,0:T(8,128)} fusion(f32[4]{0:T(128)S(1)} %compare_convert_fusion, bf16[1,4,1024,4096]{3,2,1,0:T(8,128)(2,1)} %param.10, f32[128,1024]{1,0:T(8,128)S(1)} %get-tuple-element.11), kind=kOutput, calls=%fused_computation.13 | convolution fusion | flops 4297326592 | bytes 42467344 | tf_op jit(solution)/shard_map/nk,tkd->tnd/dot_general | solution.py:19
  76.5 0.0 copy-start.3
  76.5 0.0 copy-start.4
  76.5 0.0 reduce-scatter.3.cloned.1.call-update
  76.6 0.0 reduce-scatter.5.cloned.1.call-start
  76.6 70.2 %reduce-scatter.3.cloned.1.call-done = f32[1,128,4096]{2,1,0:T(8,128)} async-done(((f32[4,128,4096]{2,1,0:T(8,128)}), f32[1,128,4096]{2,1,0:T(8,128)}) %reduce-scatter.3.cloned.1.call-update) | async-done | bytes 2097168 | tf_op jit(solution)/shard_map/reduce_scatter | solution.py:22
  146.9 0.0 reduce-scatter.5.cloned.1.call-update
  146.9 0.0 all-gather.4.cloned.1.call-start
  146.9 72.2 %reduce-scatter.5.cloned.1.call-done = f32[1,16,4096]{2,1,0:T(8,128)} async-done(((f32[1,128,4096]{2,1,0:T(8,128)}), f32[1,16,4096]{2,1,0:T(8,128)}) %reduce-scatter.5.cloned.1.call-update) | async-done | bytes 262160 | tf_op jit(solution)/shard_map/reduce_scatter | solution.py:23
  219.2 0.0 copy-done.3
  219.2 0.0 copy-done.4
  219.2 1.6 fusion.32
  220.8 0.0 all-gather.4.cloned.1.call-update
  220.8 40.6 %copy.10 = bf16[1,4,1024,4096]{2,3,1,0:T(8,128)(2,1)} copy(bf16[1,4,1024,4096]{3,2,1,0:T(8,128)(2,1)} %param.10) | data formatting | bytes 67108864 | tf_op args[4]
  261.5 0.0 copy-start.2
  261.5 0.0 all-gather.4.cloned.1.call-done
  261.5 0.0 copy-start.1
  261.5 0.1 collective-permute-start
  261.5 11.8 %fusion = f32[4,1024]{1,0:T(4,128)S(1)} fusion(bf16[1,4,1024,4096]{2,3,1,0:T(8,128)(2,1)} %copy.10), kind=kLoop, calls=%fused_computation.2 | loop fusion | flops 50327552 | bytes 33570816 | tf_op jit(solution)/shard_map/reduce_sum | solution.py:46
  273.4 0.1 multiply_reduce_fusion
  273.4 0.0 copy-done.1
  273.4 1.7 collective-permute-start.1
  275.1 0.1 broadcast_multiply_fusion
  275.2 0.0 copy-done.2
  275.2 0.1 fusion.34
  275.3 35.4 %psum.7 = f32[1,4096]{1,0:T(1,128)} all-reduce(f32[1,4096]{1,0:T(1,128)S(1)} %bitcast.81), channel_id=1, replica_groups=mesh['layer'=4,'latent'=8] {'latent'}, use_global_device_ids=true, to_apply=%region_7.8 | all-reduce | flops 4096 | bytes 32768 | tf_op jit(solution)/shard_map/psum | solution.py:25
  310.7 0.7 copy.12
  311.4 0.0 collective-permute-done
  311.4 0.2 collective-permute-start.2
  311.6 2.6 broadcast.70
  314.2 1.0 constant_dynamic-update-slice_fusion.3
  315.2 1.6 copy.13
  316.8 0.0 collective-permute-done.1
  316.8 1.6 copy.14
  318.5 1.0 constant_dynamic-update-slice_fusion.2
  319.5 1.0 constant_dynamic-update-slice_fusion.1
  320.5 5.6 %collective-permute-done.2 = bf16[1,128,4096]{2,1,0:T(8,128)(2,1)} collective-permute-done((bf16[1,128,4096]{2,1,0:T(8,128)(2,1)}, bf16[1,128,4096]{2,1,0:T(8,128)(2,1)}, u32[]{:S(2)}, u32[]{:S(2)}) %collective-permute-start.2) | collective-permute-done | bytes 1048608 | tf_op jit(solution)/shard_map/ppermute | solution.py:36
  326.1 1.6 copy.15
  327.8 1.0 constant_dynamic-update-slice_fusion
  328.8 24.5 %fusion.7 = bf16[1,4,1024,4096]{2,3,1,0:T(8,128)(2,1)} fusion(bf16[1,4,1024,4096]{2,3,1,0:T(8,128)(2,1)} %copy.10, f32[4,1024]{1,0:T(4,128)S(1)} %broadcast_multiply_fusion, bf16[4,128,4096]{1,2,0:T(8,128)(2,1)} %constant_dynamic-update-slice_fusion, pred[4]{0:T(512)(128)(4,1)S(1)} %broadcast_compare_fusion, f32[128,1024]{1,0:T(8,128)S(1)} %get-tuple-element.11), kind=kOutput, calls=%fused_computation.9 | convolution fusion | flops 4364435456 | bytes 71843840 | tf_op jit(solution)/shard_map/nk,tnd->tkd/dot_general | solution.py:58
  353.3 17.8 %fusion.40 = (f32[1024]{0:T(1024)}, bf16[128,1024]{1,0:T(8,128)(2,1)S(1)}) fusion(f32[128,1024]{1,0:T(8,128)S(1)} %get-tuple-element.11, f32[1024]{0:T(1024)S(1)} %get-tuple-element.9, bf16[1,4,1024,4096]{3,2,1,0:T(8,128)(2,1)} %param.10, bf16[4,128,4096]{1,2,0:T(8,128)(2,1)} %constant_dynamic-update-slice_fusion, pred[4]{0:T(512)(128)(4,1)S(1)} %broadcast_compare_fusion), kind=kOutput, calls=%fused_computation.46 | convolution fusion | flops 4297718784 | bytes 38543364 | tf_op jit(solution)/shard_map/tnd,tkd->nk/dot_general | solution.py:48
  371.0 0.0 copy-start
  371.0 40.5 %copy.19 = bf16[1,4,1024,4096]{3,2,1,0:T(8,128)(2,1)} copy(bf16[1,4,1024,4096]{2,3,1,0:T(8,128)(2,1)} %fusion.7) | data formatting | bytes 67108864
  411.6 0.0 copy-done
  411.6 5.6 %convert_bitcast_fusion = bf16[1,4096,1024]{1,2,0:T(8,128)(2,1)} fusion(bf16[1,128,4096]{2,1,0:T(8,128)(2,1)S(1)} %copy-done, bf16[128,1024]{1,0:T(8,128)(2,1)S(1)} %get-tuple-element.13), kind=kOutput, calls=%fused_computation.12 | convolution fusion | flops 1077936128 | bytes 9699328 | tf_op jit(solution)/shard_map/dot_general | solution.py:53
  417.2 11.9 %copy.18 = bf16[1,4096,1024]{2,1,0:T(8,128)(2,1)} copy(bf16[1,4096,1024]{1,2,0:T(8,128)(2,1)} %convert_bitcast_fusion) | data formatting | bytes 16777216
  (3 shorter events, 0.0 us)
Async XLA Ops:
  7.2 46.0 %all-gather.6.cloned.1.call-start = ((), (), s32[]{:S(2)}) async-start(), calls=%async_computation.5 | async-start | bytes 1179648 | tf_op jit(solution)/shard_map/all_gather | solution.py:13
  7.9 139.0 %reduce-scatter.3.cloned.1.call-start = ((), (), s32[]{:S(2)}) async-start(), calls=%async_computation.2 | async-start | bytes 10485760 | tf_op jit(solution)/shard_map/reduce_scatter | solution.py:22
  76.5 142.6 %copy-start.3 = (bf16[1,16,4096]{2,1,0:T(8,128)(2,1)S(1)}, bf16[1,16,4096]{2,1,0:T(8,128)(2,1)}, u32[]{:S(2)}) copy-start(bf16[1,16,4096]{2,1,0:T(8,128)(2,1)} %param.7) | copy-start | bytes 393220
  76.5 142.6 %copy-start.4 = (f32[1,4096]{1,0:T(1,128)S(1)}, f32[1,4096]{1,0:T(1,128)}, u32[]{:S(2)}) copy-start(f32[1,4096]{1,0:T(1,128)} %param.11) | copy-start | bytes 49156
  76.6 142.6 %reduce-scatter.5.cloned.1.call-start = ((), (), s32[]{:S(2)}) async-start(), calls=%async_computation.3 | async-start | bytes 2359296 | tf_op jit(solution)/shard_map/reduce_scatter | solution.py:23
  146.9 114.6 %all-gather.4.cloned.1.call-start = ((), (), s32[]{:S(2)}) async-start(), calls=%async_computation.4 | async-start | bytes 1179648 | tf_op jit(solution)/shard_map/all_gather | solution.py:27
  261.5 13.8 %copy-start.2 = (f32[1,16,4096]{2,1,0:T(8,128)S(1)}, f32[1,16,4096]{2,1,0:T(8,128)}, u32[]{:S(2)}) copy-start(f32[1,16,4096]{2,1,0:T(8,128)} %reduce-scatter.5.cloned.1.call-done) | copy-start | bytes 786436
  261.5 12.0 %copy-start.1 = (bf16[1,128,4096]{2,1,0:T(8,128)(2,1)S(1)}, bf16[1,128,4096]{2,1,0:T(8,128)(2,1)}, u32[]{:S(2)}) copy-start(bf16[1,128,4096]{2,1,0:T(8,128)(2,1)} %all-gather.4.cloned.1.call-done) | copy-start | bytes 3145732
  261.5 49.9 %collective-permute-start = (bf16[1,128,4096]{2,1,0:T(8,128)(2,1)}, bf16[1,128,4096]{2,1,0:T(8,128)(2,1)}, u32[]{:S(2)}, u32[]{:S(2)}) collective-permute-start(bf16[1,128,4096]{2,1,0:T(8,128)(2,1)} %all-gather.4.cloned.1.call-done), channel_id=1, source_target_pairs={{0,8},{8,16},{16,24},{24,0},{1,9},{9,17},{17,25},{25,1},{2,10},{10... | collective-permute-start | bytes 3145736 | tf_op jit(solution)/shard_map/ppermute | solution.py:36
  273.4 43.4 %collective-permute-start.1 = (bf16[1,128,4096]{2,1,0:T(8,128)(2,1)S(1)}, bf16[1,128,4096]{2,1,0:T(8,128)(2,1)}, u32[]{:S(2)}, u32[]{:S(2)}) collective-permute-start(bf16[1,128,4096]{2,1,0:T(8,128)(2,1)S(1)} %copy-done.1), channel_id=1, source_target_pairs={{0,24},{8,0},{16,8},{24,16},{1,25},{9,1},{17,9},{25,17},{2,26},{10... | collective-permute-start | bytes 3145736 | tf_op jit(solution)/shard_map/ppermute | solution.py:39
  311.4 14.8 %collective-permute-start.2 = (bf16[1,128,4096]{2,1,0:T(8,128)(2,1)}, bf16[1,128,4096]{2,1,0:T(8,128)(2,1)}, u32[]{:S(2)}, u32[]{:S(2)}) collective-permute-start(bf16[1,128,4096]{2,1,0:T(8,128)(2,1)} %collective-permute-done), channel_id=1, source_target_pairs={{0,8},{8,16},{16,24},{24,0},{1,9},{9,17},{17,25},{25,1},{2,10},{10... | collective-permute-start | bytes 3145736 | tf_op jit(solution)/shard_map/ppermute | solution.py:36
  371.0 40.5 %copy-start = (bf16[1,128,4096]{2,1,0:T(8,128)(2,1)S(1)}, bf16[1,128,4096]{2,1,0:T(8,128)(2,1)}, u32[]{:S(2)}) copy-start(bf16[1,128,4096]{2,1,0:T(8,128)(2,1)} %all-gather.6.cloned.1.call-done) | copy-start | bytes 3145732
Sparse Core Ops, SparseCore 0:
  10.1 42.9 all-gather.5
  76.7 70.1 reduce-scatter.2
  150.4 68.7 reduce-scatter.4
  221.7 39.2 all-gather.3
